TPU v7x, 128 devices: a whole 4x4x4 slice. The times are simulated.
128 devices in a mesh: row: 8 (over y_lo, x), col: 16 (over y_hi, z, core).
Axes of the slice: x: 4, y: 4 (y_hi: 2, y_lo: 2; y = y_hi * 2 + y_lo), z: 4, core: 2. Of those that a mesh axis runs over, the one named last changes fastest.
Arguments:
- factor_panel: bfloat16 [12288, 98304], P('row', 'col'), may hold values from -1 to 1, as said below
- normals: bfloat16 [98304, 128], P(('col', 'row')), may hold values from -6 to 6
- bond_vectors: float32 [3, 4096, 12], P(None, ('col', 'row')), may hold values from -9 to 9
- neighbours: int32 [4096, 12], P(('col', 'row')), may hold values from 0 to 175
- send_atoms: int32 [128, 16], P(('col', 'row')), may hold values from 0 to 31
- radial_weight: bfloat16 [128, 128], replicated, may hold values from -1.5 to 1.5
- radial_bias: float32 [128], replicated, may hold values from -3 to 3
- middle_weight: bfloat16 [128, 128], replicated, may hold values from -0.5 to 0.5
- middle_bias: float32 [128], replicated, may hold values from -3 to 3
- output_weight: float32 [128], replicated, may hold values from -0.5 to 0.5
Outputs:
- atom_energy: float32 [4096, 128], P(('col', 'row'))
- forces: float32 [3, 4096, 128], P(None, ('col', 'row'))
Inputs may be any that keep to these rules, and one draw needn't show every extreme that they name: `factor_panel`: entries above the factor's diagonal are zero.
All inputs are finite; a program needn't handle non-finite values.
Results may differ from a plain program's by a relative error of at most 0.0052.
Values may be sent and summed in bfloat16 or wider, within the bound.
A program may use at most 128 MiB of HBM per device.

v0:
```python
import jax
import jax.numpy as jnp
from jax import lax
from jax.sharding import PartitionSpec as P

TILE = 16


def with_halo(cells, sides, width):
    for axis, dim in sides:
        count = lax.axis_size(axis)
        head = lax.slice_in_dim(cells, 0, width, axis=dim)
        tail = lax.slice_in_dim(cells, cells.shape[dim] - width, cells.shape[dim], axis=dim)
        cells = jnp.concatenate(
            [
                lax.ppermute(tail, axis, [(i, (i + 1) % count) for i in range(count)]),
                cells,
                lax.ppermute(head, axis, [((i + 1) % count, i) for i in range(count)]),
            ],
            axis=dim,
        )
    return cells


def pair_terms(
    own_disp,
    near_disp,
    bond_block,
    radial_weight,
    radial_bias,
    middle_weight,
    middle_bias,
    output_weight,
):
    vectors = bond_block[:, :, :, None] + near_disp - own_disp[:, :, None, :]
    squared = jnp.sum(vectors * vectors, axis=0)
    count = radial_weight.shape[0]
    centres = 30.0 * jnp.arange(count, dtype=jnp.float32) / (count - 1)
    spread = 90.0 / (count - 1)
    scaled = (squared[..., None] - centres) / spread
    basis = jnp.exp(-scaled * scaled)
    flat_basis = basis.reshape(-1, count)
    flat_scaled = scaled.reshape(-1, count)
    first = jnp.tanh(
        jnp.dot(flat_basis.astype(jnp.bfloat16), radial_weight, preferred_element_type=jnp.float32)
        + radial_bias
    )
    second = jnp.tanh(
        jnp.dot(first.astype(jnp.bfloat16), middle_weight, preferred_element_type=jnp.float32)
        + middle_bias
    )
    energies = jnp.sum(second * output_weight, axis=-1)
    back_second = ((1.0 - second * second) * output_weight).astype(jnp.bfloat16)
    back_first = (
        jnp.dot(back_second, middle_weight.T, preferred_element_type=jnp.float32)
        * (1.0 - first * first)
    ).astype(jnp.bfloat16)
    radial_grad = jnp.dot(back_first, radial_weight.T, preferred_element_type=jnp.float32)
    slopes = jnp.sum(radial_grad * flat_basis * (-2.0 / spread) * flat_scaled, axis=-1)
    shape = squared.shape
    atom_part = 0.5 * jnp.sum(energies.reshape(shape), axis=1)
    force_part = 2.0 * jnp.sum(slopes.reshape(shape)[None] * vectors, axis=2)
    return (atom_part, force_part)


def per_device(
    factor_panel,
    normals,
    bond_vectors,
    neighbours,
    send_atoms,
    radial_weight,
    radial_bias,
    middle_weight,
    middle_bias,
    output_weight,
):
    samples = normals.shape[1]
    local_rows = factor_panel.shape[0]
    partial_value = jnp.dot(
        factor_panel,
        lax.all_gather(normals, "row", axis=0, tiled=True),
        preferred_element_type=jnp.float32,
    )
    col_count = lax.axis_size("col")
    col_index = lax.axis_index("col")
    slab_rows = local_rows // col_count
    total = lax.psum(partial_value, "col")
    slab = lax.dynamic_slice_in_dim(total, col_index * slab_rows, slab_rows, 0)
    rows_count = lax.axis_size("row")
    row_index = lax.axis_index("row")
    tiles = slab_rows // TILE
    whole = lax.all_gather(slab, "row", axis=0, tiled=True)
    ordered = (
        whole.reshape(rows_count, tiles, TILE, samples)
        .transpose(1, 0, 2, 3)
        .reshape(rows_count * slab_rows, samples)
    )
    domain = lax.dynamic_slice_in_dim(ordered, row_index * slab_rows, slab_rows, 0)
    domain_atoms = bond_vectors.shape[1]
    neighbour_count = bond_vectors.shape[2]
    displacements = domain.reshape(3, domain_atoms, samples)
    sent = jnp.take(displacements, send_atoms[0], axis=1)
    beside_all = with_halo(sent[None, None], (("row", 0), ("col", 1)), 1)
    halo_atoms = jnp.moveaxis(beside_all, 2, 0).reshape(3, 9 * sent.shape[1], samples)
    pool = jnp.concatenate([displacements, halo_atoms], axis=1)
    nearby = jnp.take(pool, neighbours.reshape(-1), axis=1).reshape(
        3, domain_atoms, neighbour_count, samples
    )
    block_count = domain_atoms // 8
    own_blocks = displacements.reshape(3, block_count, 8, samples).transpose(1, 0, 2, 3)
    near_blocks = nearby.reshape(3, block_count, 8, neighbour_count, samples).transpose(
        1, 0, 2, 3, 4
    )
    bond_blocks = bond_vectors.reshape(3, block_count, 8, neighbour_count).transpose(1, 0, 2, 3)
    energy_blocks, force_blocks = lax.map(
        lambda items: pair_terms(
            items[0],
            items[1],
            items[2],
            radial_weight,
            radial_bias,
            middle_weight,
            middle_bias,
            output_weight,
        ),
        (own_blocks, near_blocks, bond_blocks),
    )
    atom_energy = energy_blocks.reshape(domain_atoms, samples)
    forces = force_blocks.transpose(1, 0, 2, 3).reshape(3, domain_atoms, samples)
    return (atom_energy, forces)


def solution(mesh):
    return jax.shard_map(
        per_device,
        mesh=mesh,
        in_specs=(
            P("row", "col"),
            P(("col", "row"), None),
            P(None, ("col", "row"), None),
            P(("col", "row"), None),
            P(("col", "row"), None),
            P(),
            P(),
            P(),
            P(),
            P(),
        ),
        out_specs=(P(("col", "row"), None), P(None, ("col", "row"), None)),
        check_vma=False,
    )
```

profile of v0, /device:TPU:103, one launch (start us, length us, event | category | flops | bytes accessed | tf_op | source)
XLA Modules:
  0.0 323.6 jit_solution(1270470169724800918)
XLA Ops:
  8.0 35.4 %all-gather.2.cloned.1.call-done = bf16[6144,128]{1,0:T(8,128)(2,1)} async-done(((bf16[768,128]{1,0:T(8,128)(2,1)}), bf16[6144,128]{1,0:T(8,128)(2,1)}) %all-gather.2.cloned.1.call-update) | async-done | bytes 1572880 | tf_op jit(solution)/shard_map/all_gather | solution.py:82
  43.4 10.2 %fusion.22 = f32[1536,128]{1,0:T(8,128)} fusion(bf16[1536,6144]{1,0:T(8,128)(2,1)} %param.12, bf16[6144,128]{1,0:T(8,128)(2,1)} %all-gather.2.cloned.1.call-done), kind=kOutput, calls=%fused_computation.54 | convolution fusion | flops 2415919104 | bytes 21233664 | tf_op jit(solution)/shard_map/dot_general | solution.py:80
  53.9 147.7 %all-reduce.2.cloned.1.call-done = f32[1536,128]{1,0:T(8,128)} async-done(((f32[1536,128]{1,0:T(8,128)}), f32[1536,128]{1,0:T(8,128)}) %all-reduce.2.cloned.1.call-update) | async-done | bytes 786448 | tf_op jit(solution)/shard_map/psum | solution.py:88
  202.4 22.9 %all_gather.7 = f32[768,128]{1,0:T(8,128)S(1)} all-gather(f32[96,128]{1,0:T(8,128)S(1)} %constant_dynamic-slice_fusion.1), channel_id=1, replica_groups=mesh['row'=8,'col'=16] {'row'}, dimensions={0}, use_global_device_ids=true | all-gather | bytes 442368 | tf_op jit(solution)/shard_map/all_gather | solution.py:93
  226.1 0.9 collective-permute-start
  227.8 1.2 collective-permute-done
  228.9 2.9 collective-permute-done.1
  231.9 9.4 %collective-permute-start.2 = (f32[3,1,3,16,128]{4,2,3,1,0:T(4,128)S(1)}, f32[3,1,3,16,128]{4,2,3,1,0:T(4,128)S(1)}, u32[]{:S(2)}, u32[]{:S(2)}) collective-permute-start(f32[3,1,3,16,128]{4,2,3,1,0:T(4,128)S(1)} %pad_maximum_fusion.2), channel_id=1, source_target_pairs={{0,1},{1,2},{2,3},{3,4},{4,5},{5,6},{6,7},{7,8},{8,9},{9,10},{10,1... | collective-permute-start | bytes 221192 | tf_op jit(solution)/shard_map/ppermute | solution.py:16
  241.3 1.6 collective-permute-done.2
  242.9 6.0 %collective-permute-done.3 = f32[3,1,3,16,128]{4,2,3,1,0:T(4,128)S(1)} collective-permute-done((f32[3,1,3,16,128]{4,2,3,1,0:T(4,128)S(1)}, f32[3,1,3,16,128]{4,2,3,1,0:T(4,128)S(1)}, u32[]{:S(2)}, u32[]{:S(2)}) %collective-permute-start.3) | collective-permute-done | bytes 73760 | tf_op jit(solution)/shard_map/ppermute | solution.py:18
  249.1 2.0 gather_fusion.1
  251.4 64.7 %while.14 = (s32[]{:T(128)}, f32[4,8,128]{2,1,0:T(8,128)S(1)}, f32[4,3,8,128]{3,2,1,0:T(8,128)S(1)}, f32[4,3,8,12]{3,2,0,1:T(8,128)S(1)}, f32[4,3,8,12,128]{4,3,...) while((s32[]{:T(128)}, f32[4,8,128]{2,1,0:T(8,128)S(1)}, ...), condition=%wide.region_7.8_spmd, body=%wide.region_1.7_spmd.sunk | while | flops 1651777664 | bytes 57794740 | solution.py:116
  251.6 2.5 fusion.42
  254.0 4.5 %multiply_reduce_fusion.7 = (f32[12288]{0:T(1024)S(1)}, f32[12288,128]{1,0:T(8,128)}) fusion(f32[128]{0:T(128)S(1)} %get-tuple-element.295, f32[128]{0:T(128)S(1)} %get-tuple-element.294, bf16[128,128]{1,0:T(8,128)(2,1)S(1)} %get-tuple-element.293, f32[12288,128]{1,0:T(8,128)S(1)} %fusion.42), kind=kOutput, calls=%fused_computation.15.clone.1 | convolution fusion | flops 408932352 | bytes 12665856 | tf_op jit(solution)/shard_map/while/body/eval_jaxpr/dot_general | solution.py:49
  258.6 8.7 %fusion.43 = f32[12288]{0:T(1024)S(1)} fusion(f32[128]{0:T(128)S(1)} %iota_multiply_fusion.2, f32[12288]{0:T(1024)S(1)} %sub.114, bf16[128,128]{1,0:T(8,128)(2,1)S(1)} %get-tuple-element.291, bf16[128,128]{1,0:T(8,128)(2,1)S(1)} %get-tuple-element.293, f32[12288,128]{1,0:T(8,128)} %copy-done, f32[12288,128]{1,0:T(8,128)} %get-tuple-element.258, ...), kind=kOutput, calls=%fused_computation.23.clone.1 | convolution fusion | flops 830459904 | bytes 12747776 | tf_op jit(solution)/shard_map/while/body/eval_jaxpr/dot_general | solution.py:58
  267.8 2.5 fusion.42
  270.2 4.5 %multiply_reduce_fusion.7 = (f32[12288]{0:T(1024)S(1)}, f32[12288,128]{1,0:T(8,128)}) fusion(f32[128]{0:T(128)S(1)} %get-tuple-element.295, f32[128]{0:T(128)S(1)} %get-tuple-element.294, bf16[128,128]{1,0:T(8,128)(2,1)S(1)} %get-tuple-element.293, f32[12288,128]{1,0:T(8,128)S(1)} %fusion.42), kind=kOutput, calls=%fused_computation.15.clone.1 | convolution fusion | flops 408932352 | bytes 12665856 | tf_op jit(solution)/shard_map/while/body/eval_jaxpr/dot_general | solution.py:49
  274.8 8.7 %fusion.43 = f32[12288]{0:T(1024)S(1)} fusion(f32[128]{0:T(128)S(1)} %iota_multiply_fusion.2, f32[12288]{0:T(1024)S(1)} %sub.114, bf16[128,128]{1,0:T(8,128)(2,1)S(1)} %get-tuple-element.291, bf16[128,128]{1,0:T(8,128)(2,1)S(1)} %get-tuple-element.293, f32[12288,128]{1,0:T(8,128)} %copy-done, f32[12288,128]{1,0:T(8,128)} %get-tuple-element.258, ...), kind=kOutput, calls=%fused_computation.23.clone.1 | convolution fusion | flops 830459904 | bytes 12747776 | tf_op jit(solution)/shard_map/while/body/eval_jaxpr/dot_general | solution.py:58
  283.9 2.5 fusion.42
  286.4 4.5 %multiply_reduce_fusion.7 = (f32[12288]{0:T(1024)S(1)}, f32[12288,128]{1,0:T(8,128)}) fusion(f32[128]{0:T(128)S(1)} %get-tuple-element.295, f32[128]{0:T(128)S(1)} %get-tuple-element.294, bf16[128,128]{1,0:T(8,128)(2,1)S(1)} %get-tuple-element.293, f32[12288,128]{1,0:T(8,128)S(1)} %fusion.42), kind=kOutput, calls=%fused_computation.15.clone.1 | convolution fusion | flops 408932352 | bytes 12665856 | tf_op jit(solution)/shard_map/while/body/eval_jaxpr/dot_general | solution.py:49
  290.9 8.7 %fusion.43 = f32[12288]{0:T(1024)S(1)} fusion(f32[128]{0:T(128)S(1)} %iota_multiply_fusion.2, f32[12288]{0:T(1024)S(1)} %sub.114, bf16[128,128]{1,0:T(8,128)(2,1)S(1)} %get-tuple-element.291, bf16[128,128]{1,0:T(8,128)(2,1)S(1)} %get-tuple-element.293, f32[12288,128]{1,0:T(8,128)} %copy-done, f32[12288,128]{1,0:T(8,128)} %get-tuple-element.258, ...), kind=kOutput, calls=%fused_computation.23.clone.1 | convolution fusion | flops 830459904 | bytes 12747776 | tf_op jit(solution)/shard_map/while/body/eval_jaxpr/dot_general | solution.py:58
  300.1 2.5 fusion.42
  302.6 4.5 %multiply_reduce_fusion.7 = (f32[12288]{0:T(1024)S(1)}, f32[12288,128]{1,0:T(8,128)}) fusion(f32[128]{0:T(128)S(1)} %get-tuple-element.295, f32[128]{0:T(128)S(1)} %get-tuple-element.294, bf16[128,128]{1,0:T(8,128)(2,1)S(1)} %get-tuple-element.293, f32[12288,128]{1,0:T(8,128)S(1)} %fusion.42), kind=kOutput, calls=%fused_computation.15.clone.1 | convolution fusion | flops 408932352 | bytes 12665856 | tf_op jit(solution)/shard_map/while/body/eval_jaxpr/dot_general | solution.py:49
  307.1 8.7 %fusion.43 = f32[12288]{0:T(1024)S(1)} fusion(f32[128]{0:T(128)S(1)} %iota_multiply_fusion.2, f32[12288]{0:T(1024)S(1)} %sub.114, bf16[128,128]{1,0:T(8,128)(2,1)S(1)} %get-tuple-element.291, bf16[128,128]{1,0:T(8,128)(2,1)S(1)} %get-tuple-element.293, f32[12288,128]{1,0:T(8,128)} %copy-done, f32[12288,128]{1,0:T(8,128)} %get-tuple-element.258, ...), kind=kOutput, calls=%fused_computation.23.clone.1 | convolution fusion | flops 830459904 | bytes 12747776 | tf_op jit(solution)/shard_map/while/body/eval_jaxpr/dot_general | solution.py:58
  (98 shorter events, 5.7 us)
Async XLA Ops:
  7.2 36.2 %all-gather.2.cloned.1.call-start = ((), (), s32[]{:S(2)}) async-start(), calls=%async_computation | async-start | bytes 1769472 | tf_op jit(solution)/shard_map/all_gather | solution.py:82
  7.9 45.7 %copy-start.5 = (s32[32,12]{0,1:T(8,128)S(1)}, s32[32,12]{0,1:T(8,128)}, u32[]{:S(2)}) copy-start(s32[32,12]{0,1:T(8,128)} %param.15) | copy-start | bytes 4612
  7.9 45.9 %copy-start.8 = (s32[1,16]{1,0:T(1,128)S(1)}, s32[1,16]{1,0:T(1,128)}, u32[]{:S(2)}) copy-start(s32[1,16]{1,0:T(1,128)} %param.16) | copy-start | bytes 196
  7.9 219.7 %copy-start.2 = (f32[3,32,12]{1,2,0:T(8,128)S(1)}, f32[3,32,12]{1,2,0:T(8,128)}, u32[]{:S(2)}) copy-start(f32[3,32,12]{1,2,0:T(8,128)} %param.14) | copy-start | bytes 13828
  7.9 193.6 %all-reduce.2.cloned.1.call-start = ((), (), s32[]{:S(2)}) async-start(), calls=%async_computation.1 | async-start | bytes 1572864 | tf_op jit(solution)/shard_map/psum | solution.py:88
  53.6 197.7 %copy-start.1 = (bf16[128,128]{1,0:T(8,128)(2,1)S(1)}, bf16[128,128]{1,0:T(8,128)(2,1)}, u32[]{:S(2)}) copy-start(bf16[128,128]{1,0:T(8,128)(2,1)} %param.19) | copy-start | bytes 98308
  53.6 197.8 %copy-start.3 = (f32[128]{0:T(128)S(1)}, f32[128]{0:T(128)}, u32[]{:S(2)}) copy-start(f32[128]{0:T(128)} %param.20) | copy-start | bytes 1540
  53.6 197.8 %copy-start.4 = (f32[128]{0:T(128)S(1)}, f32[128]{0:T(128)}, u32[]{:S(2)}) copy-start(f32[128]{0:T(128)} %param.21) | copy-start | bytes 1540
  53.6 197.8 %copy-start.6 = (bf16[128,128]{1,0:T(8,128)(2,1)S(1)}, bf16[128,128]{1,0:T(8,128)(2,1)}, u32[]{:S(2)}) copy-start(bf16[128,128]{1,0:T(8,128)(2,1)} %param.17) | copy-start | bytes 98308
  53.6 197.8 %copy-start.9 = (f32[128]{0:T(128)S(1)}, f32[128]{0:T(128)}, u32[]{:S(2)}) copy-start(f32[128]{0:T(128)} %param.18) | copy-start | bytes 1540
  226.1 2.8 collective-permute-start
  227.0 4.9 %collective-permute-start.1 = (f32[1,1,3,16,128]{4,2,3,1,0:T(4,128)S(1)}, f32[1,1,3,16,128]{4,2,3,1,0:T(4,128)S(1)}, u32[]{:S(2)}, u32[]{:S(2)}) collective-permute-start(f32[1,1,3,16,128]{4,2,3,1,0:T(4,128)S(1)} %bitcast_select_fusion), channel_id=1, source_target_pairs={{16,0},{32,16},{48,32},{64,48},{80,64},{96,80},{112,96},{0,112},{1... | collective-permute-start | bytes 73736 | tf_op jit(solution)/shard_map/ppermute | solution.py:18
  231.9 11.0 %collective-permute-start.2 = (f32[3,1,3,16,128]{4,2,3,1,0:T(4,128)S(1)}, f32[3,1,3,16,128]{4,2,3,1,0:T(4,128)S(1)}, u32[]{:S(2)}, u32[]{:S(2)}) collective-permute-start(f32[3,1,3,16,128]{4,2,3,1,0:T(4,128)S(1)} %pad_maximum_fusion.2), channel_id=1, source_target_pairs={{0,1},{1,2},{2,3},{3,4},{4,5},{5,6},{6,7},{7,8},{8,9},{9,10},{10,1... | collective-permute-start | bytes 221192 | tf_op jit(solution)/shard_map/ppermute | solution.py:16
  241.3 7.7 %collective-permute-start.3 = (f32[3,1,3,16,128]{4,2,3,1,0:T(4,128)S(1)}, f32[3,1,3,16,128]{4,2,3,1,0:T(4,128)S(1)}, u32[]{:S(2)}, u32[]{:S(2)}) collective-permute-start(f32[3,1,3,16,128]{4,2,3,1,0:T(4,128)S(1)} %pad_maximum_fusion.2), channel_id=1, source_target_pairs={{1,0},{2,1},{3,2},{4,3},{5,4},{6,5},{7,6},{8,7},{9,8},{10,9},{11,1... | collective-permute-start | bytes 221192 | tf_op jit(solution)/shard_map/ppermute | solution.py:18
  254.0 4.5 %copy-start = (f32[12288,128]{1,0:T(8,128)}, f32[12288,128]{1,0:T(8,128)S(1)}, u32[]{:S(2)}) copy-start(f32[12288,128]{1,0:T(8,128)S(1)} %fusion.42) | copy-start | bytes 18874372 | tf_op jit(solution)/shard_map/while
  270.2 4.5 %copy-start = (f32[12288,128]{1,0:T(8,128)}, f32[12288,128]{1,0:T(8,128)S(1)}, u32[]{:S(2)}) copy-start(f32[12288,128]{1,0:T(8,128)S(1)} %fusion.42) | copy-start | bytes 18874372 | tf_op jit(solution)/shard_map/while
  286.4 4.5 %copy-start = (f32[12288,128]{1,0:T(8,128)}, f32[12288,128]{1,0:T(8,128)S(1)}, u32[]{:S(2)}) copy-start(f32[12288,128]{1,0:T(8,128)S(1)} %fusion.42) | copy-start | bytes 18874372 | tf_op jit(solution)/shard_map/while
  302.6 4.5 %copy-start = (f32[12288,128]{1,0:T(8,128)}, f32[12288,128]{1,0:T(8,128)S(1)}, u32[]{:S(2)}) copy-start(f32[12288,128]{1,0:T(8,128)S(1)} %fusion.42) | copy-start | bytes 18874372 | tf_op jit(solution)/shard_map/while
  316.1 0.6 copy-start.7
Sparse Core Ops, SparseCore 0:
  9.6 33.7 all-gather.1
  53.8 147.7 all-reduce.1
where the time goes:
time: 324 us
  waiting for transfers between devices  196 us (60%)
  matrix products  73.1 us (23%)
  blocking collectives  22.9 us (7%)
  between operations  14.3 us (4%)
  starting transfers between devices  11 us (3%)
  local copies, waits for them, and re-layouts  4.61 us (1%)
    psum x1, waiting for transfers between devices, per_device(): total = lax.psum(partial_value, 'col')  148 us
    all_gather x1, waiting for transfers between devices, per_device(): lax.all_gather(normals, 'row', axis=0, tiled=True)  35.4 us
    dot_general x4, matrix products, pair_terms(): jnp.dot(back_first, radial_weight.T, preferred_element_type=jnp.float32)  35 us
    all_gather x1, blocking collectives, per_device(): whole = lax.all_gather(slab, 'row', axis=0, tiled=True)  22.9 us
    dot_general x4, matrix products, pair_terms(): jnp.dot(first.astype(jnp.bfloat16), middle_weight, preferred_element_type...  18.1 us
    ppermute x2, starting transfers between devices, with_halo(): lax.ppermute(tail, axis, [(i, (i + 1) % count) for i in range(count)])  10.3 us
    dot_general x1, matrix products, per_device(): jnp.dot(factor_panel, lax.all_gather(normals, 'row', axis=0, tiled=True),...  10.2 us
    dot_general x4, matrix products, pair_terms(): jnp.dot(flat_basis.astype(jnp.bfloat16), radial_weight, preferred_element...  9.83 us
  transfers between devices with their start and end apart: 6, of which 6 were waited for; matrix products, arithmetic and copies ran while one was open for 0% of the time, Pallas kernels for 0%

commit v1 on v0

--- a/solution.py
+++ b/solution.py
@@ -4,6 +4,13 @@
 from jax.sharding import PartitionSpec as P
 
 TILE = 16
+
+
+def all_by_exchange(x, mesh_axis, dim):
+    size = lax.axis_size(mesh_axis)
+    shards = jnp.stack([x for _ in range(size)])
+    shards = lax.all_to_all(shards, mesh_axis, split_axis=0, concat_axis=0)
+    return jnp.concatenate(shards, axis=dim)
 
 
 def with_halo(cells, sides, width):
@@ -90,7 +97,7 @@
     rows_count = lax.axis_size("row")
     row_index = lax.axis_index("row")
     tiles = slab_rows // TILE
-    whole = lax.all_gather(slab, "row", axis=0, tiled=True)
+    whole = all_by_exchange(slab, "row", 0)
     ordered = (
         whole.reshape(rows_count, tiles, TILE, samples)
         .transpose(1, 0, 2, 3)

time: 324 us -> 308 us (0.951)
  blocking collectives: 22.9 us -> 0 us
  waiting for transfers between devices: 196 us -> 201 us
    all_gather x1 -> x0, blocking collectives: 22.9 us -> none  [per_device(): whole = lax.all_gather(slab, 'row', axis=0, tiled=True)]
    all_to_all x0 -> x1, starting transfers between devices: none -> 5.16 us  [all_by_exchange(): shards = lax.all_to_all(shards, mesh_axis, split_axis=0, concat_axis=0)]
    all_to_all x0 -> x1, waiting for transfers between devices: none -> 4.57 us  [all_by_exchange(): shards = lax.all_to_all(shards, mesh_axis, split_axis=0, concat_axis=0)]
    ppermute x2, starting transfers between devices: 10.3 us -> 6.71 us  [with_halo(): lax.ppermute(tail, axis, [(i, (i + 1) % count) for i in range(count)])]
  transfers between devices with their start and end apart: 6 -> 7, of which waited for: 6 -> 7; matrix products, arithmetic and copies ran while one was open for 0% -> 0% of each run, Pallas kernels for 0% -> 0%
where the time goes in v1:
time: 308 us
  waiting for transfers between devices  201 us (65%)
  matrix products  73 us (24%)
  between operations  14.3 us (5%)
  starting transfers between devices  12 us (4%)
  local copies, waits for them, and re-layouts  5.39 us (2%)
    psum x1, waiting for transfers between devices, per_device(): total = lax.psum(partial_value, 'col')  148 us
    all_gather x1, waiting for transfers between devices, per_device(): lax.all_gather(normals, 'row', axis=0, tiled=True)  35.4 us
    dot_general x4, matrix products, pair_terms(): jnp.dot(back_first, radial_weight.T, preferred_element_type=jnp.float32)  35 us
    dot_general x4, matrix products, pair_terms(): jnp.dot(first.astype(jnp.bfloat16), middle_weight, preferred_element_type...  18 us
    dot_general x1, matrix products, per_device(): jnp.dot(factor_panel, lax.all_gather(normals, 'row', axis=0, tiled=True),...  10.2 us
    ppermute x2, waiting for transfers between devices, with_halo(): lax.ppermute(head, axis, [((i + 1) % count, i) for i in range(count)])  9.87 us
    dot_general x4, matrix products, pair_terms(): jnp.dot(flat_basis.astype(jnp.bfloat16), radial_weight, preferred_element...  9.82 us
    ppermute x2, starting transfers between devices, with_halo(): lax.ppermute(tail, axis, [(i, (i + 1) % count) for i in range(count)])  6.71 us
  transfers between devices with their start and end apart: 7, of which 7 were waited for; matrix products, arithmetic and copies ran while one was open for 0% of the time, Pallas kernels for 0%

profile of v1, /device:TPU:103, one launch (start us, length us, event | category | flops | bytes accessed | tf_op | source)
XLA Modules:
  0.0 307.8 jit_solution(4524308585044127769)
XLA Ops:
  8.0 35.4 %all-gather.2.cloned.1.call-done = bf16[6144,128]{1,0:T(8,128)(2,1)} async-done(((bf16[768,128]{1,0:T(8,128)(2,1)}), bf16[6144,128]{1,0:T(8,128)(2,1)}) %all-gather.2.cloned.1.call-update) | async-done | bytes 1572880 | tf_op jit(solution)/shard_map/all_gather | solution.py:89
  43.4 10.2 %fusion.22 = f32[1536,128]{1,0:T(8,128)} fusion(bf16[1536,6144]{1,0:T(8,128)(2,1)} %param.12, bf16[6144,128]{1,0:T(8,128)(2,1)} %all-gather.2.cloned.1.call-done), kind=kOutput, calls=%fused_computation.54 | convolution fusion | flops 2415919104 | bytes 21233664 | tf_op jit(solution)/shard_map/dot_general | solution.py:87
  53.7 147.9 %all-reduce.2.cloned.1.call-done = f32[1536,128]{1,0:T(8,128)} async-done(((f32[1536,128]{1,0:T(8,128)}), f32[1536,128]{1,0:T(8,128)}) %all-reduce.2.cloned.1.call-update) | async-done | bytes 786448 | tf_op jit(solution)/shard_map/psum | solution.py:95
  203.2 5.2 %all-to-all-start = ((f32[8,96,128]{2,1,0:T(8,128)}), f32[8,96,128]{2,1,0:T(8,128)S(1)}, u32[]{:S(2)}, u32[]{:S(2)}) async-start(f32[8,96,128]{2,1,0:T(8,128)} %stack.2), calls=%async_computation | async-start | bytes 786432 | tf_op jit(solution)/shard_map/all_to_all | solution.py:12
  208.6 4.6 %all-to-all-done = f32[8,96,128]{2,1,0:T(8,128)S(1)} async-done(((f32[8,96,128]{2,1,0:T(8,128)}), f32[8,96,128]{2,1,0:T(8,128)S(1)}, u32[]{:S(2)}, u32[]{:S(2)}) %all-to-all-start) | async-done | bytes 393248 | tf_op jit(solution)/shard_map/all_to_all | solution.py:12
  213.9 2.1 collective-permute-start
  217.0 3.9 %collective-permute-done.1 = f32[1,1,3,16,128]{4,2,3,1,0:T(4,128)S(1)} collective-permute-done((f32[1,1,3,16,128]{4,2,3,1,0:T(4,128)S(1)}, f32[1,1,3,16,128]{4,2,3,1,0:T(4,128)S(1)}, u32[]{:S(2)}, u32[]{:S(2)}) %collective-permute-start.1) | collective-permute-done | bytes 24608 | tf_op jit(solution)/shard_map/ppermute | solution.py:25
  220.9 4.6 %collective-permute-start.2 = (f32[3,1,3,16,128]{4,2,3,1,0:T(4,128)S(1)}, f32[3,1,3,16,128]{4,2,3,1,0:T(4,128)S(1)}, u32[]{:S(2)}, u32[]{:S(2)}) collective-permute-start(f32[3,1,3,16,128]{4,2,3,1,0:T(4,128)S(1)} %pad_maximum_fusion.2), channel_id=1, source_target_pairs={{0,1},{1,2},{2,3},{3,4},{4,5},{5,6},{6,7},{7,8},{8,9},{9,10},{10,1... | collective-permute-start | bytes 221192 | tf_op jit(solution)/shard_map/ppermute | solution.py:23
  225.6 1.6 collective-permute-done.2
  227.2 6.0 %collective-permute-done.3 = f32[3,1,3,16,128]{4,2,3,1,0:T(4,128)S(1)} collective-permute-done((f32[3,1,3,16,128]{4,2,3,1,0:T(4,128)S(1)}, f32[3,1,3,16,128]{4,2,3,1,0:T(4,128)S(1)}, u32[]{:S(2)}, u32[]{:S(2)}) %collective-permute-start.3) | collective-permute-done | bytes 73760 | tf_op jit(solution)/shard_map/ppermute | solution.py:25
  233.4 2.0 gather_fusion.1
  235.6 64.7 %while.14 = (s32[]{:T(128)}, f32[4,8,128]{2,1,0:T(8,128)S(1)}, f32[4,3,8,128]{3,2,1,0:T(8,128)S(1)}, f32[4,3,8,12]{3,2,0,1:T(8,128)S(1)}, f32[4,3,8,12,128]{4,3,...) while((s32[]{:T(128)}, f32[4,8,128]{2,1,0:T(8,128)S(1)}, ...), condition=%wide.region_7.8_spmd, body=%wide.region_1.7_spmd.sunk | while | flops 1651777664 | bytes 57794740 | solution.py:123
  235.8 2.5 fusion.42
  238.3 4.5 %multiply_reduce_fusion.7 = (f32[12288]{0:T(1024)S(1)}, f32[12288,128]{1,0:T(8,128)}) fusion(f32[128]{0:T(128)S(1)} %get-tuple-element.295, f32[128]{0:T(128)S(1)} %get-tuple-element.294, bf16[128,128]{1,0:T(8,128)(2,1)S(1)} %get-tuple-element.293, f32[12288,128]{1,0:T(8,128)S(1)} %fusion.42), kind=kOutput, calls=%fused_computation.15.clone.1 | convolution fusion | flops 408932352 | bytes 12665856 | tf_op jit(solution)/shard_map/while/body/eval_jaxpr/dot_general | solution.py:56
  242.8 8.7 %fusion.43 = f32[12288]{0:T(1024)S(1)} fusion(f32[128]{0:T(128)S(1)} %iota_multiply_fusion.2, f32[12288]{0:T(1024)S(1)} %sub.114, bf16[128,128]{1,0:T(8,128)(2,1)S(1)} %get-tuple-element.291, bf16[128,128]{1,0:T(8,128)(2,1)S(1)} %get-tuple-element.293, f32[12288,128]{1,0:T(8,128)} %copy-done, f32[12288,128]{1,0:T(8,128)} %get-tuple-element.258, ...), kind=kOutput, calls=%fused_computation.23.clone.1 | convolution fusion | flops 830459904 | bytes 12747776 | tf_op jit(solution)/shard_map/while/body/eval_jaxpr/dot_general | solution.py:65
  252.0 2.5 fusion.42
  254.5 4.5 %multiply_reduce_fusion.7 = (f32[12288]{0:T(1024)S(1)}, f32[12288,128]{1,0:T(8,128)}) fusion(f32[128]{0:T(128)S(1)} %get-tuple-element.295, f32[128]{0:T(128)S(1)} %get-tuple-element.294, bf16[128,128]{1,0:T(8,128)(2,1)S(1)} %get-tuple-element.293, f32[12288,128]{1,0:T(8,128)S(1)} %fusion.42), kind=kOutput, calls=%fused_computation.15.clone.1 | convolution fusion | flops 408932352 | bytes 12665856 | tf_op jit(solution)/shard_map/while/body/eval_jaxpr/dot_general | solution.py:56
  259.0 8.7 %fusion.43 = f32[12288]{0:T(1024)S(1)} fusion(f32[128]{0:T(128)S(1)} %iota_multiply_fusion.2, f32[12288]{0:T(1024)S(1)} %sub.114, bf16[128,128]{1,0:T(8,128)(2,1)S(1)} %get-tuple-element.291, bf16[128,128]{1,0:T(8,128)(2,1)S(1)} %get-tuple-element.293, f32[12288,128]{1,0:T(8,128)} %copy-done, f32[12288,128]{1,0:T(8,128)} %get-tuple-element.258, ...), kind=kOutput, calls=%fused_computation.23.clone.1 | convolution fusion | flops 830459904 | bytes 12747776 | tf_op jit(solution)/shard_map/while/body/eval_jaxpr/dot_general | solution.py:65
  268.2 2.5 fusion.42
  270.6 4.5 %multiply_reduce_fusion.7 = (f32[12288]{0:T(1024)S(1)}, f32[12288,128]{1,0:T(8,128)}) fusion(f32[128]{0:T(128)S(1)} %get-tuple-element.295, f32[128]{0:T(128)S(1)} %get-tuple-element.294, bf16[128,128]{1,0:T(8,128)(2,1)S(1)} %get-tuple-element.293, f32[12288,128]{1,0:T(8,128)S(1)} %fusion.42), kind=kOutput, calls=%fused_computation.15.clone.1 | convolution fusion | flops 408932352 | bytes 12665856 | tf_op jit(solution)/shard_map/while/body/eval_jaxpr/dot_general | solution.py:56
  275.1 8.7 %fusion.43 = f32[12288]{0:T(1024)S(1)} fusion(f32[128]{0:T(128)S(1)} %iota_multiply_fusion.2, f32[12288]{0:T(1024)S(1)} %sub.114, bf16[128,128]{1,0:T(8,128)(2,1)S(1)} %get-tuple-element.291, bf16[128,128]{1,0:T(8,128)(2,1)S(1)} %get-tuple-element.293, f32[12288,128]{1,0:T(8,128)} %copy-done, f32[12288,128]{1,0:T(8,128)} %get-tuple-element.258, ...), kind=kOutput, calls=%fused_computation.23.clone.1 | convolution fusion | flops 830459904 | bytes 12747776 | tf_op jit(solution)/shard_map/while/body/eval_jaxpr/dot_general | solution.py:65
  284.3 2.5 fusion.42
  286.8 4.5 %multiply_reduce_fusion.7 = (f32[12288]{0:T(1024)S(1)}, f32[12288,128]{1,0:T(8,128)}) fusion(f32[128]{0:T(128)S(1)} %get-tuple-element.295, f32[128]{0:T(128)S(1)} %get-tuple-element.294, bf16[128,128]{1,0:T(8,128)(2,1)S(1)} %get-tuple-element.293, f32[12288,128]{1,0:T(8,128)S(1)} %fusion.42), kind=kOutput, calls=%fused_computation.15.clone.1 | convolution fusion | flops 408932352 | bytes 12665856 | tf_op jit(solution)/shard_map/while/body/eval_jaxpr/dot_general | solution.py:56
  291.3 8.7 %fusion.43 = f32[12288]{0:T(1024)S(1)} fusion(f32[128]{0:T(128)S(1)} %iota_multiply_fusion.2, f32[12288]{0:T(1024)S(1)} %sub.114, bf16[128,128]{1,0:T(8,128)(2,1)S(1)} %get-tuple-element.291, bf16[128,128]{1,0:T(8,128)(2,1)S(1)} %get-tuple-element.293, f32[12288,128]{1,0:T(8,128)} %copy-done, f32[12288,128]{1,0:T(8,128)} %get-tuple-element.258, ...), kind=kOutput, calls=%fused_computation.23.clone.1 | convolution fusion | flops 830459904 | bytes 12747776 | tf_op jit(solution)/shard_map/while/body/eval_jaxpr/dot_general | solution.py:65
  (100 shorter events, 6.7 us)
Async XLA Ops:
  7.2 36.2 %all-gather.2.cloned.1.call-start = ((), (), s32[]{:S(2)}) async-start(), calls=%async_computation.1 | async-start | bytes 1769472 | tf_op jit(solution)/shard_map/all_gather | solution.py:89
  7.9 45.7 %copy-start.8 = (s32[1,16]{1,0:T(1,128)S(1)}, s32[1,16]{1,0:T(1,128)}, u32[]{:S(2)}) copy-start(s32[1,16]{1,0:T(1,128)} %param.16) | copy-start | bytes 196
  7.9 200.4 %copy-start.5 = (s32[32,12]{0,1:T(8,128)S(1)}, s32[32,12]{0,1:T(8,128)}, u32[]{:S(2)}) copy-start(s32[32,12]{0,1:T(8,128)} %param.15) | copy-start | bytes 4612
  7.9 208.1 %copy-start.2 = (f32[3,32,12]{1,2,0:T(8,128)S(1)}, f32[3,32,12]{1,2,0:T(8,128)}, u32[]{:S(2)}) copy-start(f32[3,32,12]{1,2,0:T(8,128)} %param.14) | copy-start | bytes 13828
  7.9 193.7 %all-reduce.2.cloned.1.call-start = ((), (), s32[]{:S(2)}) async-start(), calls=%async_computation.2 | async-start | bytes 1572864 | tf_op jit(solution)/shard_map/psum | solution.py:95
  53.6 182.0 %copy-start.1 = (bf16[128,128]{1,0:T(8,128)(2,1)S(1)}, bf16[128,128]{1,0:T(8,128)(2,1)}, u32[]{:S(2)}) copy-start(bf16[128,128]{1,0:T(8,128)(2,1)} %param.19) | copy-start | bytes 98308
  53.6 182.0 %copy-start.3 = (f32[128]{0:T(128)S(1)}, f32[128]{0:T(128)}, u32[]{:S(2)}) copy-start(f32[128]{0:T(128)} %param.20) | copy-start | bytes 1540
  53.6 182.0 %copy-start.4 = (f32[128]{0:T(128)S(1)}, f32[128]{0:T(128)}, u32[]{:S(2)}) copy-start(f32[128]{0:T(128)} %param.21) | copy-start | bytes 1540
  53.6 182.0 %copy-start.6 = (bf16[128,128]{1,0:T(8,128)(2,1)S(1)}, bf16[128,128]{1,0:T(8,128)(2,1)}, u32[]{:S(2)}) copy-start(bf16[128,128]{1,0:T(8,128)(2,1)} %param.17) | copy-start | bytes 98308
  53.6 182.0 %copy-start.9 = (f32[128]{0:T(128)S(1)}, f32[128]{0:T(128)}, u32[]{:S(2)}) copy-start(f32[128]{0:T(128)} %param.18) | copy-start | bytes 1540
  203.2 10.0 %all-to-all-start = ((f32[8,96,128]{2,1,0:T(8,128)}), f32[8,96,128]{2,1,0:T(8,128)S(1)}, u32[]{:S(2)}, u32[]{:S(2)}) async-start(f32[8,96,128]{2,1,0:T(8,128)} %stack.2), calls=%async_computation | async-start | bytes 786432 | tf_op jit(solution)/shard_map/all_to_all | solution.py:12
  213.9 3.1 %collective-permute-start = (f32[1,1,3,16,128]{4,2,3,1,0:T(4,128)S(1)}, f32[1,1,3,16,128]{4,2,3,1,0:T(4,128)S(1)}, u32[]{:S(2)}, u32[]{:S(2)}) collective-permute-start(f32[1,1,3,16,128]{4,2,3,1,0:T(4,128)S(1)} %bitcast_select_fusion), channel_id=1, source_target_pairs={{0,16},{16,32},{32,48},{48,64},{64,80},{80,96},{96,112},{112,0},{1... | collective-permute-start | bytes 73736 | tf_op jit(solution)/shard_map/ppermute | solution.py:23
  216.0 4.9 %collective-permute-start.1 = (f32[1,1,3,16,128]{4,2,3,1,0:T(4,128)S(1)}, f32[1,1,3,16,128]{4,2,3,1,0:T(4,128)S(1)}, u32[]{:S(2)}, u32[]{:S(2)}) collective-permute-start(f32[1,1,3,16,128]{4,2,3,1,0:T(4,128)S(1)} %bitcast_select_fusion), channel_id=1, source_target_pairs={{16,0},{32,16},{48,32},{64,48},{80,64},{96,80},{112,96},{0,112},{1... | collective-permute-start | bytes 73736 | tf_op jit(solution)/shard_map/ppermute | solution.py:25
  220.9 6.3 %collective-permute-start.2 = (f32[3,1,3,16,128]{4,2,3,1,0:T(4,128)S(1)}, f32[3,1,3,16,128]{4,2,3,1,0:T(4,128)S(1)}, u32[]{:S(2)}, u32[]{:S(2)}) collective-permute-start(f32[3,1,3,16,128]{4,2,3,1,0:T(4,128)S(1)} %pad_maximum_fusion.2), channel_id=1, source_target_pairs={{0,1},{1,2},{2,3},{3,4},{4,5},{5,6},{6,7},{7,8},{8,9},{9,10},{10,1... | collective-permute-start | bytes 221192 | tf_op jit(solution)/shard_map/ppermute | solution.py:23
  225.5 7.7 %collective-permute-start.3 = (f32[3,1,3,16,128]{4,2,3,1,0:T(4,128)S(1)}, f32[3,1,3,16,128]{4,2,3,1,0:T(4,128)S(1)}, u32[]{:S(2)}, u32[]{:S(2)}) collective-permute-start(f32[3,1,3,16,128]{4,2,3,1,0:T(4,128)S(1)} %pad_maximum_fusion.2), channel_id=1, source_target_pairs={{1,0},{2,1},{3,2},{4,3},{5,4},{6,5},{7,6},{8,7},{9,8},{10,9},{11,1... | collective-permute-start | bytes 221192 | tf_op jit(solution)/shard_map/ppermute | solution.py:25
  238.3 4.5 %copy-start = (f32[12288,128]{1,0:T(8,128)}, f32[12288,128]{1,0:T(8,128)S(1)}, u32[]{:S(2)}) copy-start(f32[12288,128]{1,0:T(8,128)S(1)} %fusion.42) | copy-start | bytes 18874372 | tf_op jit(solution)/shard_map/while
  254.4 4.5 %copy-start = (f32[12288,128]{1,0:T(8,128)}, f32[12288,128]{1,0:T(8,128)S(1)}, u32[]{:S(2)}) copy-start(f32[12288,128]{1,0:T(8,128)S(1)} %fusion.42) | copy-start | bytes 18874372 | tf_op jit(solution)/shard_map/while
  270.6 4.5 %copy-start = (f32[12288,128]{1,0:T(8,128)}, f32[12288,128]{1,0:T(8,128)S(1)}, u32[]{:S(2)}) copy-start(f32[12288,128]{1,0:T(8,128)S(1)} %fusion.42) | copy-start | bytes 18874372 | tf_op jit(solution)/shard_map/while
  286.8 4.5 %copy-start = (f32[12288,128]{1,0:T(8,128)}, f32[12288,128]{1,0:T(8,128)S(1)}, u32[]{:S(2)}) copy-start(f32[12288,128]{1,0:T(8,128)S(1)} %fusion.42) | copy-start | bytes 18874372 | tf_op jit(solution)/shard_map/while
  300.3 0.6 copy-start.7
Sparse Core Ops, SparseCore 0:
  9.6 33.7 all-gather.1
  53.8 147.7 all-reduce.1
